TPU v7x, 128 devices: a whole 4x4x4 slice. The times are simulated.
128 devices in a mesh: section: 2 (over z_lo), patch: 4 (over y), shard: 16 (over z_hi, x, core).
Axes of the slice: x: 4, y: 4, z: 4 (z_hi: 2, z_lo: 2; z = z_hi * 2 + z_lo), core: 2. Of those that a mesh axis runs over, the one named last changes fastest.
Arguments:
- hidden: bfloat16 [32, 1024, 2432], P('shard', 'patch'), may hold values from -6 to 6
- text_kv: bfloat16 [2, 32, 154, 2432], P('section', 'shard'), may hold values from -6 to 6, as said below
- stale_kv: bfloat16 [2, 32, 1024, 2432], P('section', 'shard', 'patch'), may hold values from -6 to 6, as said below
- modulation: float32 [2, 32, 3, 2432], P('section', 'shard'), may hold values from -3 to 3
- score_gain: float32 [2, 64], P('section'), may hold values from 1.5 to 4
- qkv_weight: bfloat16 [2, 2432, 3648], P('section', 'shard'), may hold values from -0.125 to 0.125
- out_weight: bfloat16 [2, 1216, 2432], P('section', None, 'shard'), may hold values from -0.15625 to 0.15625
- final_mod: float32 [32, 2, 2432], P('shard'), may hold values from -3 to 3
- final_weight: bfloat16 [2432, 64], replicated, may hold values from -0.125 to 0.125
- latent: float32 [32, 1024, 64], P('shard', ('patch', 'section')), may hold values from -6 to 6
- step_index: int32 [32], P('shard'), may hold values from 0 to 27
Outputs:
- new_kv: bfloat16 [2, 32, 1024, 2432], P('section', 'shard', 'patch')
- latent_next: float32 [32, 1024, 64], P('shard', ('patch', 'section'))
- denoised: float32 [32, 1024, 64], P('shard', ('patch', 'section'))
Inputs may be any that keep to these rules, and one draw needn't show every extreme that they name: `text_kv`: in every row the first 1216 columns are 19 heads of 64 key features, each head with mean square one up to bfloat16 rounding. `stale_kv`: in every row the first 1216 columns are 19 heads of 64 key features, each head with mean square one up to bfloat16 rounding.
All inputs are finite; a program needn't handle non-finite values.
Results may differ from a plain program's by a relative error of at most 0.008.
Values may be sent and summed in bfloat16 or wider, within the bound.
No kernel may reach another device: no remote copies, remote signals or barrier semaphores. Data moves between devices by JAX's collectives and lax.ppermute only.
A program may use at most 192 MiB of HBM per device.

v0:
```python
import math
import jax
import jax.numpy as jnp
from jax import lax
from jax.sharding import PartitionSpec as P

HEAD = 64
NSTEPS = 28
eps_norm = 1e-06
flow_shift = 3.0


def passed_along(value, axis, steps):
    count = lax.axis_size(axis)
    first, last = (max(0, -steps), min(count, count - steps))
    return lax.ppermute(value, axis, [(source, source + steps) for source in range(first, last)])


def spread(array, axis, root):
    mine = lax.axis_index(axis) == root
    return lax.psum(jnp.where(mine, array, jnp.zeros_like(array)), axis)


def sigma_of(step):
    s = 1.0 - step.astype(jnp.float32) / NSTEPS
    return flow_shift * s / (1.0 + (flow_shift - 1.0) * s)


def modulated(xf, shift, scale):
    mean = jnp.mean(xf, -1, keepdims=True)
    cent = xf - mean
    var = jnp.mean(cent * cent, -1, keepdims=True)
    return cent * lax.rsqrt(var + eps_norm) * (1.0 + scale) + shift


def attend_one(query, keys_all, width, heads):
    count = keys_all.shape[0]
    keys = keys_all[:, :width].reshape(count, heads, HEAD)
    values = keys_all[:, width:].reshape(count, heads, HEAD)
    scores = jnp.einsum("qhe,khe->hqk", query, keys, preferred_element_type=jnp.float32)
    expo = jnp.exp(scores)
    total = jnp.sum(expo, -1)
    weights = expo.astype(jnp.bfloat16)
    mixed = jnp.einsum("hqk,khe->qhe", weights, values, preferred_element_type=jnp.float32)
    mixed = mixed / jnp.transpose(total)[:, :, None]
    return mixed.reshape(query.shape[0], width).astype(jnp.bfloat16)


def run_layer(x, stale_all, text_one, mod_one, gain, w_qkv, w_out, patch_index):
    requests, rows = (x.shape[0], x.shape[1])
    width = w_out.shape[0]
    heads = width // HEAD
    xf = x.astype(jnp.float32)
    normed = modulated(xf, mod_one[:, 0:1, :], mod_one[:, 1:2, :]).astype(jnp.bfloat16)
    proj_in = jnp.einsum("rid,dc->ric", normed, w_qkv, preferred_element_type=jnp.float32)
    q = proj_in[..., :width].reshape(requests, rows, heads, HEAD)
    k = proj_in[..., width : 2 * width].reshape(requests, rows, heads, HEAD)
    v = proj_in[..., 2 * width :]
    q_hat = q * lax.rsqrt(jnp.mean(q * q, -1, keepdims=True) + eps_norm)
    k_hat = k * lax.rsqrt(jnp.mean(k * k, -1, keepdims=True) + eps_norm)
    fresh = jnp.concatenate(
        [k_hat.reshape(requests, rows, width).astype(jnp.bfloat16), v.astype(jnp.bfloat16)], -1
    )
    query = (q_hat * gain / math.sqrt(HEAD)).astype(jnp.bfloat16)
    mixed = lax.dynamic_update_slice_in_dim(stale_all, fresh, patch_index * rows, 1)
    keys_all = jnp.concatenate([text_one, mixed], 1)

    def per_request(pair):
        return attend_one(pair[0], pair[1], width, heads)

    attn = lax.map(per_request, (query, keys_all))
    proj = jnp.einsum("riw,wd->rid", attn, w_out, preferred_element_type=jnp.float32)
    x_next = (xf + mod_one[:, 2:3, :] * proj).astype(jnp.bfloat16)
    return (x_next, fresh)


def on_device(
    hidden,
    text_kv,
    stale_kv,
    modulation,
    score_gain,
    qkv_weight,
    out_weight,
    final_mod,
    final_weight,
    latent,
    step_index,
):
    w_qkv, w_out = (
        lax.all_gather(qkv_weight[0], "shard", axis=0, tiled=True),
        lax.all_gather(out_weight[0], "shard", axis=1, tiled=True),
    )
    stale_all = lax.all_gather(stale_kv[0], "patch", axis=1, tiled=True)
    section = lax.axis_index("section")
    patch_index = lax.axis_index("patch")

    def compute(x):
        return run_layer(
            x, stale_all, text_kv[0], modulation[0], score_gain[0], w_qkv, w_out, patch_index
        )

    def passing(x):
        return (x, jnp.zeros(stale_kv.shape[1:], jnp.bfloat16))

    first, fresh_first = lax.cond(section == 0, compute, passing, hidden)
    arrived = passed_along(first, "section", 1)
    last, fresh_last = lax.cond(section == 1, compute, passing, arrived)
    fresh = jnp.where(section == 0, fresh_first, fresh_last)
    final = modulated(last.astype(jnp.float32), final_mod[:, 0:1, :], final_mod[:, 1:2, :]).astype(
        jnp.bfloat16
    )
    velocity = jnp.einsum("rid,dc->ric", final, final_weight, preferred_element_type=jnp.float32)
    half = latent.shape[1]
    shared = spread(velocity.astype(jnp.bfloat16), "section", 1).astype(velocity.dtype)
    velocity_mine = lax.dynamic_slice_in_dim(shared, section * half, half, 1)
    sig = sigma_of(step_index)[:, None, None]
    sig_next = sigma_of(step_index + 1)[:, None, None]
    latent_next = latent + (sig_next - sig) * velocity_mine
    denoised = latent - sig * velocity_mine
    return (fresh[None], latent_next, denoised)


def solution(mesh):
    in_specs = (
        P("shard", "patch", None),
        P("section", "shard", None, None),
        P("section", "shard", "patch", None),
        P("section", "shard", None, None),
        P("section", None),
        P("section", "shard", None),
        P("section", None, "shard"),
        P("shard", None, None),
        P(),
        P("shard", ("patch", "section"), None),
        P("shard"),
    )
    out_specs = (
        P("section", "shard", "patch", None),
        P("shard", ("patch", "section"), None),
        P("shard", ("patch", "section"), None),
    )
    return jax.shard_map(
        on_device, mesh=mesh, in_specs=in_specs, out_specs=out_specs, check_vma=False
    )
```

profile of v0, /device:TPU:1, one launch (start us, length us, event | category | flops | bytes accessed | tf_op | source)
XLA Modules:
  0.0 642.9 jit_solution(3232019068005679391)
XLA Ops:
  8.0 4.5 copy.28
  13.3 64.7 %all-gather.11.cloned.1.call-done = bf16[1,1216,2432]{1,2,0:T(8,128)(2,1)} async-done(((bf16[1,1216,152]{1,2,0:T(8,128)(2,1)}), bf16[1,1216,2432]{1,2,0:T(8,128)(2,1)}) %all-gather.11.cloned.1.call-update) | async-done | bytes 5914640 | tf_op jit(solution)/shard_map/all_gather | solution.py:92
  78.0 100.0 %all-gather.9.cloned.1.call-done = bf16[1,2,1024,2432]{2,3,1,0:T(8,128)(2,1)} async-done(((bf16[1,2,256,2432]{2,3,1,0:T(8,128)(2,1)}), bf16[1,2,1024,2432]{2,3,1,0:T(8,128)(2,1)}) %all-gather.9.cloned.1.call-update) | async-done | bytes 9961488 | tf_op jit(solution)/shard_map/all_gather | solution.py:94
  177.9 120.4 %all-gather.7.cloned.1.call-done = bf16[1,2432,3648]{2,1,0:T(8,128)(2,1)} async-done(((bf16[1,152,3648]{2,1,0:T(8,128)(2,1)}), bf16[1,2432,3648]{2,1,0:T(8,128)(2,1)}) %all-gather.7.cloned.1.call-update) | async-done | bytes 17743888 | tf_op jit(solution)/shard_map/all_gather | solution.py:91
  298.4 129.6 %conditional.2 = (bf16[2,256,2432]{2,1,0:T(8,128)(2,1)S(1)}, bf16[2,256,2432]{2,1,0:T(8,128)(2,1)}) conditional(s32[]{:T(128)} %convert_element_type.88, bf16[2,256,2432]{2,1,0:T(8,128)(2,1)S(1)} %copy-done.2, (bf16[2,256,2432]{2,1,0:T(8,128)(2,1)S(1)}, f32[1,2,3,2432]{3,1,2,0:T(2,128)S(1)}, bf16[2432,3648]{1,0:T(8,128)(2,1)}, f32[1,64]{1,0:T(1,128)S(1)}, ...), branch_computations={%region_0.0_spmd, %region_1.9_spmd} | conditional | flops 13646128128 | bytes 220811024 | solution.py:106
  300.2 16.5 %fusion.6 = f32[2,256,3648]{1,2,0:T(8,128)} fusion(bf16[2432,3648]{1,0:T(8,128)(2,1)} %get-tuple-element.139, bf16[2,256,2432]{2,1,0:T(8,128)(2,1)S(1)} %get-tuple-element.71, f32[2,2432]{1,0:T(2,128)S(1)} %get-tuple-element.182, f32[2,2432]{1,0:T(2,128)S(1)} %get-tuple-element.183, f32[2,256]{1,0:T(2,128)S(1)} %add_rsqrt_fusion.2, ...), kind=kOutput, calls=%fused_computation.11 | convolution fusion | flops 9092333568 | bytes 27748352 | tf_op jit(solution)/shard_map/cond/branch_1_fun/rid,dc->ric/dot_general | solution.py:55
  316.7 3.3 slice_multiply_fusion
  322.1 4.7 fusion.76
  329.6 8.8 %copy.62 = bf16[2,1024,2432]{1,2,0:T(8,128)(2,1)} copy(bf16[2,1024,2432]{1,2,0:T(8,128)(2,1)} %get-tuple-element.74) | data formatting | bytes 19922944 | tf_op jit(solution)/shard_map/cond
  338.4 4.3 pad_maximum_fusion.1
  342.7 5.8 copy.30
  348.5 13.1 %pad_maximum_fusion = bf16[2,1178,2432]{1,2,0:T(8,128)(2,1)} fusion(bf16[2,1024,2432]{1,2,0:T(8,128)(2,1)} %get-tuple-element.180, bf16[2,154,2432]{1,2,0:T(8,128)(2,1)} %bitcast.147), kind=kLoop, calls=%fused_computation.13 | loop fusion | flops 22919168 | bytes 22919168 | tf_op jit(solution)/shard_map/cond/branch_1_fun/concatenate | solution.py:66
  363.5 52.4 %while.18 = (s32[]{:T(128)}, bf16[2,256,1216]{1,2,0:T(8,128)(2,1)}, bf16[2,1178,2432]{1,2,0:T(8,128)(2,1)}, bf16[2,256,19,64]{1,3,2,0:T(8,128)(2,1)}, s32[]{:T(128)}) while((s32[]{:T(128)}, bf16[2,256,1216]{1,2,0:T(8,128)(2,1)}, bf16[2,1178,2432]{1,2,0:T(8,128)(2,1)}, bf16[2,256,19,64]{1,3,2,0:T(8,128)(2,1)}, s32[]{:T(128)}) %tuple.88), condition=%wide.region_8.8_spmd, body=%wide.region_6.7_spmd.sunk | while | flops 1478904064 | bytes 82245984 | solution.py:71
  364.0 3.2 dynamic-slice_bitcast_fusion.5
  368.4 9.7 %exponential_reduce_fusion.5 = (f32[19,256]{1,0:T(8,128)S(1)}, f32[19,256,1178]{1,2,0:T(8,128)}) fusion(bf16[1178,19,64]{0,2,1:T(8,128)(2,1)S(1)} %bitcast.134, bf16[2,256,19,64]{1,3,2,0:T(8,128)(2,1)S(1)} %copy-done.5, s32[]{:T(128)} %get-tuple-element.287), kind=kOutput, calls=%fused_computation.clone.1 | convolution fusion | flops 739138304 | bytes 26674180 | tf_op jit(solution)/shard_map/cond/branch_1_fun/while/body/eval_jaxpr/qhe,khe->hqk/dot_general | solution.py:40
  378.1 10.9 %divide_convert_fusion.5 = bf16[256,19,64]{0,2,1:T(8,128)(2,1)S(1)} fusion(bf16[1178,19,64]{0,2,1:T(8,128)(2,1)S(1)} %bitcast.136, f32[19,256,1178]{1,2,0:T(8,128)} %get-tuple-element.265, f32[256,19]{0,1:T(8,128)S(1)} %bitcast.150), kind=kOutput, calls=%fused_computation.5.clone.1 | convolution fusion | flops 739765760 | bytes 26426112 | tf_op jit(solution)/shard_map/cond/branch_1_fun/while/body/eval_jaxpr/hqk,khe->qhe/dot_general | solution.py:44
  394.4 9.7 %exponential_reduce_fusion.5 = (f32[19,256]{1,0:T(8,128)S(1)}, f32[19,256,1178]{1,2,0:T(8,128)}) fusion(bf16[1178,19,64]{0,2,1:T(8,128)(2,1)S(1)} %bitcast.134, bf16[2,256,19,64]{1,3,2,0:T(8,128)(2,1)S(1)} %copy-done.5, s32[]{:T(128)} %get-tuple-element.287), kind=kOutput, calls=%fused_computation.clone.1 | convolution fusion | flops 739138304 | bytes 26674180 | tf_op jit(solution)/shard_map/cond/branch_1_fun/while/body/eval_jaxpr/qhe,khe->hqk/dot_general | solution.py:40
  404.1 10.9 %divide_convert_fusion.5 = bf16[256,19,64]{0,2,1:T(8,128)(2,1)S(1)} fusion(bf16[1178,19,64]{0,2,1:T(8,128)(2,1)S(1)} %bitcast.136, f32[19,256,1178]{1,2,0:T(8,128)} %get-tuple-element.265, f32[256,19]{0,1:T(8,128)S(1)} %bitcast.150), kind=kOutput, calls=%fused_computation.5.clone.1 | convolution fusion | flops 739765760 | bytes 26426112 | tf_op jit(solution)/shard_map/cond/branch_1_fun/while/body/eval_jaxpr/hqk,khe->qhe/dot_general | solution.py:44
  415.9 7.6 %fusion.19 = bf16[2,256,2432]{2,1,0:T(8,128)(2,1)S(1)} fusion(bf16[2,256,2432]{2,1,0:T(8,128)(2,1)S(1)} %get-tuple-element.71, bf16[2,256,1216]{1,2,0:T(8,128)(2,1)} %get-tuple-element.78, bf16[1216,2432]{0,1:T(8,128)(2,1)} %get-tuple-element.144, f32[2,2432]{1,0:T(2,128)S(1)} %copy-done.10), kind=kOutput, calls=%fused_computation.26 | convolution fusion | flops 3033268224 | bytes 12160000 | tf_op jit(solution)/shard_map/cond/branch_1_fun/riw,wd->rid/dot_general | solution.py:72
  423.5 4.3 copy.46
  432.2 52.4 %collective-permute-done = bf16[2,256,2432]{2,1,0:T(8,128)(2,1)S(1)} collective-permute-done((bf16[2,256,2432]{2,1,0:T(8,128)(2,1)}, bf16[2,256,2432]{2,1,0:T(8,128)(2,1)S(1)}, u32[]{:S(2)}, u32[]{:S(2)}) %collective-permute-start) | collective-permute-done | bytes 2490400 | tf_op jit(solution)/shard_map/ppermute | solution.py:16
  484.6 4.3 conditional.3
  492.0 3.4 select_bitcast_fusion
  495.5 138.9 %all-reduce.2.cloned.1.call-done = bf16[2,256,64]{1,2,0:T(8,128)(2,1)} async-done(((bf16[2,256,64]{1,2,0:T(8,128)(2,1)}), bf16[2,256,64]{1,2,0:T(8,128)(2,1)}) %all-reduce.2.cloned.1.call-update) | async-done | bytes 65552 | tf_op jit(solution)/shard_map/psum | solution.py:21
  (68 shorter events, 27.9 us)
Async XLA Ops:
  7.2 483.0 %copy-start = (bf16[2432,64]{0,1:T(8,128)(2,1)S(1)}, bf16[2432,64]{0,1:T(8,128)(2,1)}, u32[]{:S(2)}) copy-start(bf16[2432,64]{0,1:T(8,128)(2,1)} %param.27) | copy-start | bytes 933892
  7.2 70.8 %all-gather.11.cloned.1.call-start = ((), (), s32[]{:S(2)}) async-start(), calls=%async_computation.3 | async-start | bytes 6615040 | tf_op jit(solution)/shard_map/all_gather | solution.py:92
  7.9 290.4 %copy-start.2 = (bf16[2,256,2432]{2,1,0:T(8,128)(2,1)S(1)}, bf16[2,256,2432]{2,1,0:T(8,128)(2,1)}, u32[]{:S(2)}) copy-start(bf16[2,256,2432]{2,1,0:T(8,128)(2,1)} %param.19) | copy-start | bytes 7471108
  7.9 290.4 %copy-start.7 = (f32[1,2,3,2432]{3,1,2,0:T(2,128)S(1)}, f32[1,2,3,2432]{3,1,2,0:T(2,128)}, u32[]{:S(2)}) copy-start(f32[1,2,3,2432]{3,1,2,0:T(2,128)} %param.22) | copy-start | bytes 175108
  7.9 290.4 %copy-start.14 = (f32[1,64]{1,0:T(1,128)S(1)}, f32[1,64]{1,0:T(1,128)}, u32[]{:S(2)}) copy-start(f32[1,64]{1,0:T(1,128)} %param.23) | copy-start | bytes 772
  7.9 170.0 %all-gather.9.cloned.1.call-start = ((), (), s32[]{:S(2)}) async-start(), calls=%async_computation.2 | async-start | bytes 12451840 | tf_op jit(solution)/shard_map/all_gather | solution.py:94
  12.5 285.9 %all-gather.7.cloned.1.call-start = ((), (), s32[]{:S(2)}) async-start(), calls=%async_computation.1 | async-start | bytes 19183616 | tf_op jit(solution)/shard_map/all_gather | solution.py:91
  13.2 621.2 %all-reduce.2.cloned.1.call-start = ((), (), s32[]{:S(2)}) async-start(), calls=%async_computation | async-start | bytes 131072 | tf_op jit(solution)/shard_map/psum | solution.py:21
  298.4 132.5 %copy-start.17 = (s32[2]{0:T(128)S(1)}, s32[2]{0:T(128)}, u32[]{:S(2)}) copy-start(s32[2]{0:T(128)} %param.29) | copy-start | bytes 28
  298.4 133.1 %copy-start.9 = (f32[2,2,2432]{2,1,0:T(2,128)S(1)}, f32[2,2,2432]{2,1,0:T(2,128)}, u32[]{:S(2)}) copy-start(f32[2,2,2432]{2,1,0:T(2,128)} %param.26) | copy-start | bytes 116740
  348.5 13.1 %copy-start.3 = (f32[2,256,1216]{1,2,0:T(8,128)S(1)}, f32[2,256,1216]{1,2,0:T(8,128)}, u32[]{:S(2)}) copy-start(f32[2,256,1216]{1,2,0:T(8,128)} %get-tuple-element.177) | copy-start | bytes 7471108 | tf_op jit(solution)/shard_map/cond
  363.5 52.4 %copy-start.10 = (f32[2,2432]{1,0:T(2,128)S(1)}, f32[2,2432]{1,0:T(2,128)}, u32[]{:S(2)}) copy-start(f32[2,2432]{1,0:T(2,128)} %get-tuple-element.181) | copy-start | bytes 58372 | tf_op jit(solution)/shard_map/cond
  367.1 1.3 copy-start.5
  393.1 1.3 copy-start.5
  428.0 1.5 copy-start.1
  429.4 55.1 %collective-permute-start = (bf16[2,256,2432]{2,1,0:T(8,128)(2,1)}, bf16[2,256,2432]{2,1,0:T(8,128)(2,1)S(1)}, u32[]{:S(2)}, u32[]{:S(2)}) collective-permute-start(bf16[2,256,2432]{2,1,0:T(8,128)(2,1)} %copy-done.1), channel_id=1, source_target_pairs={{0,64},{1,65},{2,66},{3,67},{4,68},{5,69},{6,70},{7,71},{8,72},{9,... | collective-permute-start | bytes 7471112 | tf_op jit(solution)/shard_map/ppermute | solution.py:16
  488.9 1.2 copy-start.12
  488.9 1.2 copy-start.13
  492.0 142.4 %copy-start.8 = (f32[2,128,64]{1,2,0:T(8,128)S(1)}, f32[2,128,64]{1,2,0:T(8,128)}, u32[]{:S(2)}) copy-start(f32[2,128,64]{1,2,0:T(8,128)} %param.28) | copy-start | bytes 196612
  492.0 142.4 %copy-start.15 = (f32[2]{0:T(128)S(1)}, f32[2]{0:T(128)}, u32[]{:S(2)}) copy-start(f32[2]{0:T(128)} %get-tuple-element.171) | copy-start | bytes 28
  492.0 142.4 %copy-start.16 = (f32[2]{0:T(128)S(1)}, f32[2]{0:T(128)}, u32[]{:S(2)}) copy-start(f32[2]{0:T(128)} %get-tuple-element.172) | copy-start | bytes 28
Sparse Core Ops, SparseCore 0:
  10.4 67.5 all-gather.10
  80.2 97.6 all-gather.8
  180.5 117.8 all-gather.6
  492.1 142.2 all-reduce.1
where the time goes:
time: 652 us; the launch traced here: 643 us
  waiting for transfers between devices  478 us (73%)
  matrix products  67.2 us (10%)
  local copies, waits for them, and re-layouts  40.7 us (6%)
  other arithmetic  37.8 us (6%)
  between operations  14.4 us (2%)
    psum x1, waiting for transfers between devices, spread(): return lax.psum(jnp.where(mine, array, jnp.zeros_like(array)), axis)  139 us
    all_gather x1, waiting for transfers between devices, on_device(): lax.all_gather(qkv_weight[0], 'shard', axis=0, tiled=True)  120 us
    all_gather x1, waiting for transfers between devices, on_device(): stale_all = lax.all_gather(stale_kv[0], 'patch', axis=1, tiled=True)  100 us
    all_gather x1, waiting for transfers between devices, on_device(): lax.all_gather(out_weight[0], 'shard', axis=1, tiled=True)  64.7 us
    ppermute x1, waiting for transfers between devices, passed_along(): lax.ppermute(value, axis, [(source, source + steps) for source in range(f...  52.4 us
    dot_general x2, matrix products, attend_one(): jnp.einsum('hqk,khe->qhe', weights, values, preferred_element_type=jnp.fl...  21.8 us
    dot_general x2, matrix products, attend_one(): jnp.einsum('qhe,khe->hqk', query, keys, preferred_element_type=jnp.float32)  19.4 us
    dot_general x1, matrix products, run_layer(): jnp.einsum('rid,dc->ric', normed, w_qkv, preferred_element_type=jnp.float32)  16.5 us
  transfers between devices with their start and end apart: 5, of which 5 were waited for; matrix products, arithmetic and copies ran while one was open for 1% of the time, Pallas kernels for 0%

commit v1 on v0

--- a/solution.py
+++ b/solution.py
@@ -91,7 +91,14 @@
         lax.all_gather(qkv_weight[0], "shard", axis=0, tiled=True),
         lax.all_gather(out_weight[0], "shard", axis=1, tiled=True),
     )
-    stale_all = lax.all_gather(stale_kv[0], "patch", axis=1, tiled=True)
+    ring = [stale_kv[0]]
+    for hop in range(3):
+        ring.append(lax.ppermute(ring[-1], "patch", [(dev, (dev + 1) % 4) for dev in range(4)]))
+    stale_all = jnp.roll(
+        jnp.concatenate(ring[::-1], axis=1),
+        (lax.axis_index("patch") + 1) * ring[0].shape[1],
+        axis=1,
+    )
     section = lax.axis_index("section")
     patch_index = lax.axis_index("patch")
 

time: 652 us -> 561 us (0.86)
  waiting for transfers between devices: 478 us -> 359 us
  local copies, waits for them, and re-layouts: 40.7 us -> 70.4 us
    ppermute x0 -> x3, waiting for transfers between devices: none -> 165 us  [on_device(): lax.ppermute(ring[-1], 'patch', [(dev, (dev + 1) % 4) for dev in range(4)])]
    all_gather x1, waiting for transfers between devices: 120 us -> 0.01 us  [on_device(): lax.all_gather(qkv_weight[0], 'shard', axis=0, tiled=True)]
    all_gather x1 -> x0, waiting for transfers between devices: 100 us -> none  [on_device(): stale_all = lax.all_gather(stale_kv[0], 'patch', axis=1, tiled=True)]
    all_gather x1, waiting for transfers between devices: 64.7 us -> 0.01 us  [on_device(): lax.all_gather(out_weight[0], 'shard', axis=1, tiled=True)]
    unnamed x26 -> x37, local copies, waits for them, and re-layouts: 6.62 us -> 25.6 us
    dynamic_slice x0 -> x1, local copies, waits for them, and re-layouts: none -> 8.88 us  [on_device(): jnp.roll(jnp.concatenate(ring[::-1], axis=1), (lax.axis_index('patch') +...]
  transfers between devices with their start and end apart: 5 -> 7, of which waited for: 5 -> 5; matrix products, arithmetic and copies ran while one was open for 1% -> 7% of each run, Pallas kernels for 0% -> 0%
where the time goes in v1:
time: 561 us; the launch traced here: 556 us
  waiting for transfers between devices  359 us (64%)
  local copies, waits for them, and re-layouts  70.4 us (13%)
  matrix products  67.2 us (12%)
  other arithmetic  37.8 us (7%)
  between operations  14.1 us (3%)
    ppermute x3, waiting for transfers between devices, on_device(): lax.ppermute(ring[-1], 'patch', [(dev, (dev + 1) % 4) for dev in range(4)])  165 us
    psum x1, waiting for transfers between devices, spread(): return lax.psum(jnp.where(mine, array, jnp.zeros_like(array)), axis)  143 us
    ppermute x1, waiting for transfers between devices, passed_along(): lax.ppermute(value, axis, [(source, source + steps) for source in range(f...  49.4 us
    unnamed x37, local copies, waits for them, and re-layouts  25.6 us
    dot_general x2, matrix products, attend_one(): jnp.einsum('hqk,khe->qhe', weights, values, preferred_element_type=jnp.fl...  21.8 us
    dot_general x2, matrix products, attend_one(): jnp.einsum('qhe,khe->hqk', query, keys, preferred_element_type=jnp.float32)  19.3 us
    dot_general x1, matrix products, run_layer(): jnp.einsum('rid,dc->ric', normed, w_qkv, preferred_element_type=jnp.float32)  16.5 us
    concatenate x1, other arithmetic, run_layer(): keys_all = jnp.concatenate([text_one, mixed], 1)  13.1 us
  transfers between devices with their start and end apart: 7, of which 5 were waited for; matrix products, arithmetic and copies ran while one was open for 7% of the time, Pallas kernels for 0%

profile of v1, /device:TPU:1, one launch (start us, length us, event | category | flops | bytes accessed | tf_op | source)
XLA Modules:
  0.0 556.2 jit_solution(1447221498787377249)
XLA Ops:
  14.1 55.1 %collective-permute-done = bf16[2,256,2432]{1,2,0:T(8,128)(2,1)S(1)} collective-permute-done((bf16[2,256,2432]{1,2,0:T(8,128)(2,1)S(1)}, bf16[2,256,2432]{1,2,0:T(8,128)(2,1)S(1)}, u32[]{:S(2)}, u32[]{:S(2)}) %collective-permute-start) | collective-permute-done | bytes 2490400 | tf_op jit(solution)/shard_map/ppermute | solution.py:96
  70.6 55.5 %collective-permute-done.1 = bf16[2,256,2432]{1,2,0:T(8,128)(2,1)} collective-permute-done((bf16[2,256,2432]{1,2,0:T(8,128)(2,1)S(1)}, bf16[2,256,2432]{1,2,0:T(8,128)(2,1)}, u32[]{:S(2)}, u32[]{:S(2)}) %collective-permute-start.1) | collective-permute-done | bytes 2490400 | tf_op jit(solution)/shard_map/ppermute | solution.py:96
  126.1 54.8 %collective-permute-done.2 = bf16[2,256,2432]{1,2,0:T(8,128)(2,1)} collective-permute-done((bf16[2,256,2432]{1,2,0:T(8,128)(2,1)}, bf16[2,256,2432]{1,2,0:T(8,128)(2,1)}, u32[]{:S(2)}, u32[]{:S(2)}) %collective-permute-start.2) | collective-permute-done | bytes 2490400 | tf_op jit(solution)/shard_map/ppermute | solution.py:96
  180.9 3.6 constant_dynamic-update-slice_fusion.11
  184.5 3.5 constant_dynamic-update-slice_fusion.10
  201.5 8.9 %constant_dynamic-slice_fusion = bf16[2,1024,2432]{1,2,0:T(8,128)(2,1)} fusion(bf16[2,2048,2432]{1,2,0:T(8,128)(2,1)} %constant_dynamic-update-slice_fusion.4, s32[]{:T(128)S(6)} %select_n.40), kind=kLoop, calls=%fused_computation.126 | loop fusion | bytes 19922948 | tf_op jit(solution)/shard_map/jit(_roll_dynamic)/dynamic_slice | solution.py:97
  210.4 129.7 %conditional.2 = (bf16[2,256,2432]{2,1,0:T(8,128)(2,1)S(1)}, bf16[2,256,2432]{2,1,0:T(8,128)(2,1)}) conditional(s32[]{:T(128)} %convert_element_type.88, bf16[2,256,2432]{2,1,0:T(8,128)(2,1)S(1)} %copy-done.2, (bf16[2,256,2432]{2,1,0:T(8,128)(2,1)S(1)}, f32[1,2,3,2432]{3,1,2,0:T(2,128)S(1)}, bf16[2432,3648]{1,0:T(8,128)(2,1)}, f32[1,64]{1,0:T(1,128)S(1)}, ...), branch_computations={%region_0.1_spmd, %region_1.9_spmd} | conditional | flops 13646128128 | bytes 220811024 | solution.py:113
  212.4 16.5 %fusion.6 = f32[2,256,3648]{1,2,0:T(8,128)} fusion(bf16[2432,3648]{1,0:T(8,128)(2,1)} %get-tuple-element.139, bf16[2,256,2432]{2,1,0:T(8,128)(2,1)S(1)} %get-tuple-element.71, f32[2,2432]{1,0:T(2,128)S(1)} %get-tuple-element.182, f32[2,2432]{1,0:T(2,128)S(1)} %get-tuple-element.183, f32[2,256]{1,0:T(2,128)S(1)} %add_rsqrt_fusion.2, ...), kind=kOutput, calls=%fused_computation.11 | convolution fusion | flops 9092333568 | bytes 27748352 | tf_op jit(solution)/shard_map/cond/branch_1_fun/rid,dc->ric/dot_general | solution.py:55
  234.3 4.6 fusion.76
  241.8 8.8 %copy.62 = bf16[2,1024,2432]{1,2,0:T(8,128)(2,1)} copy(bf16[2,1024,2432]{1,2,0:T(8,128)(2,1)} %get-tuple-element.74) | data formatting | bytes 19922944 | tf_op jit(solution)/shard_map/cond
  250.6 4.3 pad_maximum_fusion.1
  254.9 5.8 %copy.30 = bf16[1,2,154,2432]{2,3,1,0:T(8,128)(2,1)} copy(bf16[1,2,154,2432]{3,1,2,0:T(2,128)(2,1)} %get-tuple-element.141) | data formatting | bytes 2996224 | tf_op jit(solution)/shard_map
  260.7 13.1 %pad_maximum_fusion = bf16[2,1178,2432]{1,2,0:T(8,128)(2,1)} fusion(bf16[2,1024,2432]{1,2,0:T(8,128)(2,1)} %get-tuple-element.180, bf16[2,154,2432]{1,2,0:T(8,128)(2,1)} %bitcast.148), kind=kLoop, calls=%fused_computation.13 | loop fusion | flops 22919168 | bytes 22919168 | tf_op jit(solution)/shard_map/cond/branch_1_fun/concatenate | solution.py:66
  275.7 52.1 %while.18 = (s32[]{:T(128)}, bf16[2,256,1216]{1,2,0:T(8,128)(2,1)}, bf16[2,1178,2432]{1,2,0:T(8,128)(2,1)}, bf16[2,256,19,64]{1,3,2,0:T(8,128)(2,1)}, s32[]{:T(128)}) while((s32[]{:T(128)}, bf16[2,256,1216]{1,2,0:T(8,128)(2,1)}, bf16[2,1178,2432]{1,2,0:T(8,128)(2,1)}, bf16[2,256,19,64]{1,3,2,0:T(8,128)(2,1)}, s32[]{:T(128)}) %tuple.88), condition=%wide.region_8.8_spmd, body=%wide.region_6.7_spmd.sunk | while | flops 1478904064 | bytes 82245984 | solution.py:71
  280.4 9.7 %exponential_reduce_fusion.5 = (f32[19,256]{1,0:T(8,128)S(1)}, f32[19,256,1178]{1,2,0:T(8,128)}) fusion(bf16[1178,19,64]{0,2,1:T(8,128)(2,1)S(1)} %bitcast.136, bf16[2,256,19,64]{1,3,2,0:T(8,128)(2,1)S(1)} %copy-done.5, s32[]{:T(128)} %get-tuple-element.287), kind=kOutput, calls=%fused_computation.clone.1 | convolution fusion | flops 739138304 | bytes 26674180 | tf_op jit(solution)/shard_map/cond/branch_1_fun/while/body/eval_jaxpr/qhe,khe->hqk/dot_general | solution.py:40
  290.0 10.9 %divide_convert_fusion.5 = bf16[256,19,64]{0,2,1:T(8,128)(2,1)S(1)} fusion(bf16[1178,19,64]{0,2,1:T(8,128)(2,1)S(1)} %bitcast.138, f32[19,256,1178]{1,2,0:T(8,128)} %get-tuple-element.265, f32[256,19]{0,1:T(8,128)S(1)} %bitcast.151), kind=kOutput, calls=%fused_computation.5.clone.1 | convolution fusion | flops 739765760 | bytes 26426112 | tf_op jit(solution)/shard_map/cond/branch_1_fun/while/body/eval_jaxpr/hqk,khe->qhe/dot_general | solution.py:44
  306.3 9.7 %exponential_reduce_fusion.5 = (f32[19,256]{1,0:T(8,128)S(1)}, f32[19,256,1178]{1,2,0:T(8,128)}) fusion(bf16[1178,19,64]{0,2,1:T(8,128)(2,1)S(1)} %bitcast.136, bf16[2,256,19,64]{1,3,2,0:T(8,128)(2,1)S(1)} %copy-done.5, s32[]{:T(128)} %get-tuple-element.287), kind=kOutput, calls=%fused_computation.clone.1 | convolution fusion | flops 739138304 | bytes 26674180 | tf_op jit(solution)/shard_map/cond/branch_1_fun/while/body/eval_jaxpr/qhe,khe->hqk/dot_general | solution.py:40
  316.0 10.9 %divide_convert_fusion.5 = bf16[256,19,64]{0,2,1:T(8,128)(2,1)S(1)} fusion(bf16[1178,19,64]{0,2,1:T(8,128)(2,1)S(1)} %bitcast.138, f32[19,256,1178]{1,2,0:T(8,128)} %get-tuple-element.265, f32[256,19]{0,1:T(8,128)S(1)} %bitcast.151), kind=kOutput, calls=%fused_computation.5.clone.1 | convolution fusion | flops 739765760 | bytes 26426112 | tf_op jit(solution)/shard_map/cond/branch_1_fun/while/body/eval_jaxpr/hqk,khe->qhe/dot_general | solution.py:44
  327.8 7.6 %fusion.19 = bf16[2,256,2432]{2,1,0:T(8,128)(2,1)S(1)} fusion(bf16[2,256,2432]{2,1,0:T(8,128)(2,1)S(1)} %get-tuple-element.71, bf16[2,256,1216]{1,2,0:T(8,128)(2,1)} %get-tuple-element.78, bf16[1216,2432]{0,1:T(8,128)(2,1)} %get-tuple-element.144, f32[2,2432]{1,0:T(2,128)S(1)} %copy-done.12), kind=kOutput, calls=%fused_computation.26 | convolution fusion | flops 3033268224 | bytes 12160000 | tf_op jit(solution)/shard_map/cond/branch_1_fun/riw,wd->rid/dot_general | solution.py:72
  335.4 4.3 copy.46
  344.3 49.4 %collective-permute-done.3 = bf16[2,256,2432]{2,1,0:T(8,128)(2,1)S(1)} collective-permute-done((bf16[2,256,2432]{2,1,0:T(8,128)(2,1)}, bf16[2,256,2432]{2,1,0:T(8,128)(2,1)S(1)}, u32[]{:S(2)}, u32[]{:S(2)}) %collective-permute-start.3) | collective-permute-done | bytes 2490400 | tf_op jit(solution)/shard_map/ppermute | solution.py:16
  393.7 4.3 conditional.3
  401.2 3.4 select_bitcast_fusion
  404.6 143.3 %all-reduce.2.cloned.1.call-done = bf16[2,256,64]{1,2,0:T(8,128)(2,1)} async-done(((bf16[2,256,64]{1,2,0:T(8,128)(2,1)}), bf16[2,256,64]{1,2,0:T(8,128)(2,1)}) %all-reduce.2.cloned.1.call-update) | async-done | bytes 65552 | tf_op jit(solution)/shard_map/psum | solution.py:21
  (84 shorter events, 54.7 us)
Async XLA Ops:
  7.2 392.1 %copy-start = (bf16[2432,64]{0,1:T(8,128)(2,1)S(1)}, bf16[2432,64]{0,1:T(8,128)(2,1)}, u32[]{:S(2)}) copy-start(bf16[2432,64]{0,1:T(8,128)(2,1)} %param.27) | copy-start | bytes 933892
  7.2 203.2 %all-gather.7.cloned.1.call-start = ((), (), s32[]{:S(2)}) async-start(), calls=%async_computation.2 | async-start | bytes 6615040 | tf_op jit(solution)/shard_map/all_gather | solution.py:92
  7.9 202.4 %all-gather.5.cloned.1.call-start = ((), (), s32[]{:S(2)}) async-start(), calls=%async_computation.1 | async-start | bytes 19183616 | tf_op jit(solution)/shard_map/all_gather | solution.py:91
  8.7 539.3 %all-reduce.2.cloned.1.call-start = ((), (), s32[]{:S(2)}) async-start(), calls=%async_computation | async-start | bytes 131072 | tf_op jit(solution)/shard_map/psum | solution.py:21
  11.9 57.3 %collective-permute-start = (bf16[2,256,2432]{1,2,0:T(8,128)(2,1)S(1)}, bf16[2,256,2432]{1,2,0:T(8,128)(2,1)S(1)}, u32[]{:S(2)}, u32[]{:S(2)}) collective-permute-start(bf16[2,256,2432]{1,2,0:T(8,128)(2,1)S(1)} %bitcast.142), channel_id=1, source_target_pairs={{0,16},{16,32},{32,48},{48,0},{1,17},{17,33},{33,49},{49,1},{2,18}... | collective-permute-start | bytes 7471112 | tf_op jit(solution)/shard_map/ppermute | solution.py:96
  69.2 1.4 copy-start.7
  70.6 55.5 %collective-permute-start.1 = (bf16[2,256,2432]{1,2,0:T(8,128)(2,1)S(1)}, bf16[2,256,2432]{1,2,0:T(8,128)(2,1)}, u32[]{:S(2)}, u32[]{:S(2)}) collective-permute-start(bf16[2,256,2432]{1,2,0:T(8,128)(2,1)S(1)} %collective-permute-done), channel_id=1, source_target_pairs={{0,16},{16,32},{32,48},{48,0},{1,17},{17,33},{33,49},{49,1},{2,18}... | collective-permute-start | bytes 7471112 | tf_op jit(solution)/shard_map/ppermute | solution.py:96
  126.1 54.8 %collective-permute-start.2 = (bf16[2,256,2432]{1,2,0:T(8,128)(2,1)}, bf16[2,256,2432]{1,2,0:T(8,128)(2,1)}, u32[]{:S(2)}, u32[]{:S(2)}) collective-permute-start(bf16[2,256,2432]{1,2,0:T(8,128)(2,1)} %collective-permute-done.1), channel_id=1, source_target_pairs={{0,16},{16,32},{32,48},{48,0},{1,17},{17,33},{33,49},{49,1},{2,18}... | collective-permute-start | bytes 7471112 | tf_op jit(solution)/shard_map/ppermute | solution.py:96
  184.5 3.5 copy-start.8
  201.5 8.9 %copy-start.2 = (bf16[2,256,2432]{2,1,0:T(8,128)(2,1)S(1)}, bf16[2,256,2432]{2,1,0:T(8,128)(2,1)}, u32[]{:S(2)}) copy-start(bf16[2,256,2432]{2,1,0:T(8,128)(2,1)} %param.19) | copy-start | bytes 7471108
  201.5 8.9 %copy-start.9 = (f32[1,2,3,2432]{3,1,2,0:T(2,128)S(1)}, f32[1,2,3,2432]{3,1,2,0:T(2,128)}, u32[]{:S(2)}) copy-start(f32[1,2,3,2432]{3,1,2,0:T(2,128)} %param.22) | copy-start | bytes 175108
  201.5 8.9 %copy-start.16 = (f32[1,64]{1,0:T(1,128)S(1)}, f32[1,64]{1,0:T(1,128)}, u32[]{:S(2)}) copy-start(f32[1,64]{1,0:T(1,128)} %param.23) | copy-start | bytes 772
  210.4 132.7 %copy-start.19 = (s32[2]{0:T(128)S(1)}, s32[2]{0:T(128)}, u32[]{:S(2)}) copy-start(s32[2]{0:T(128)} %param.29) | copy-start | bytes 28
  210.4 133.3 %copy-start.11 = (f32[2,2,2432]{2,1,0:T(2,128)S(1)}, f32[2,2,2432]{2,1,0:T(2,128)}, u32[]{:S(2)}) copy-start(f32[2,2,2432]{2,1,0:T(2,128)} %param.26) | copy-start | bytes 116740
  260.7 13.1 %copy-start.3 = (f32[2,256,1216]{1,2,0:T(8,128)S(1)}, f32[2,256,1216]{1,2,0:T(8,128)}, u32[]{:S(2)}) copy-start(f32[2,256,1216]{1,2,0:T(8,128)} %get-tuple-element.177) | copy-start | bytes 7471108 | tf_op jit(solution)/shard_map/cond
  275.7 52.1 %copy-start.12 = (f32[2,2432]{1,0:T(2,128)S(1)}, f32[2,2432]{1,0:T(2,128)}, u32[]{:S(2)}) copy-start(f32[2,2432]{1,0:T(2,128)} %get-tuple-element.181) | copy-start | bytes 58372 | tf_op jit(solution)/shard_map/cond
  279.1 1.3 copy-start.5
  305.0 1.3 copy-start.5
  340.1 1.5 copy-start.1
  341.6 52.1 %collective-permute-start.3 = (bf16[2,256,2432]{2,1,0:T(8,128)(2,1)}, bf16[2,256,2432]{2,1,0:T(8,128)(2,1)S(1)}, u32[]{:S(2)}, u32[]{:S(2)}) collective-permute-start(bf16[2,256,2432]{2,1,0:T(8,128)(2,1)} %copy-done.1), channel_id=1, source_target_pairs={{0,64},{1,65},{2,66},{3,67},{4,68},{5,69},{6,70},{7,71},{8,72},{9,... | collective-permute-start | bytes 7471112 | tf_op jit(solution)/shard_map/ppermute | solution.py:16
  398.0 1.2 copy-start.14
  401.2 146.8 %copy-start.10 = (f32[2,128,64]{1,2,0:T(8,128)S(1)}, f32[2,128,64]{1,2,0:T(8,128)}, u32[]{:S(2)}) copy-start(f32[2,128,64]{1,2,0:T(8,128)} %param.28) | copy-start | bytes 196612
  401.2 146.8 %copy-start.17 = (f32[2]{0:T(128)S(1)}, f32[2]{0:T(128)}, u32[]{:S(2)}) copy-start(f32[2]{0:T(128)} %get-tuple-element.171) | copy-start | bytes 28
  401.2 146.8 %copy-start.18 = (f32[2]{0:T(128)S(1)}, f32[2]{0:T(128)}, u32[]{:S(2)}) copy-start(f32[2]{0:T(128)} %get-tuple-element.172) | copy-start | bytes 28
  (1 other events, 1.2 us)
Sparse Core Ops, SparseCore 0:
  10.4 67.5 all-gather.6
  80.5 114.4 all-gather.4
  401.3 146.6 all-reduce.1
